TPU v7x, 32 devices: a whole 2x2x4 slice. The times are simulated.
32 devices in a mesh: dp: 8 (over z, y), fsdp: 4 (over x, core).
Axes of the slice: x: 2, y: 2, z: 4, core: 2. Of those that a mesh axis runs over, the one named last changes fastest.
Arguments:
- pixels: bfloat16 [8, 512, 192], P('dp', 'fsdp'), may hold values from -6 to 6
- targets: bfloat16 [8, 512, 192], P('dp', 'fsdp'), may hold values from 2 to 6
- valid_mask: int32 [8, 512, 192], P('dp', 'fsdp'), may hold values 0 or 1
- lat_weight: float32 [8, 512], P('dp', 'fsdp'), may hold values from 0.1 to 1
- segment_ids: int32 [8, 512], P('dp'), may hold values from 0 to 3, never falling along the last dimension, each value on 1 to 256 neighbouring positions
- present_vars: int32 [8, 48], P('dp'), may hold values from 0 to 1, as said below
- lead_index: int32 [8], P('dp'), may hold values from 0 to 7
- step_count: int32 [1], replicated, may hold values from 1 to 20
- w_agg: float32 [1024, 3072], P(('dp', 'fsdp')), may hold values from -0.1875 to 0.1875
- w_attn: float32 [1024, 4096], P(('dp', 'fsdp')), may hold values from -0.1875 to 0.1875
- w_mlp: float32 [1024, 8192], P(('dp', 'fsdp')), may hold values from -0.1875 to 0.1875
- w_io: float32 [1024, 944], P(('dp', 'fsdp')), may hold values from -3 to 3
- w_small: float32 [1024, 9], P(('dp', 'fsdp')), may hold values from 0.5 to 1.5
- m_agg: float32 [1024, 3072], P(('dp', 'fsdp')), may hold values from -0.00390625 to 0.00390625
- m_attn: float32 [1024, 4096], P(('dp', 'fsdp')), may hold values from -0.00390625 to 0.00390625
- m_mlp: float32 [1024, 8192], P(('dp', 'fsdp')), may hold values from -0.00390625 to 0.00390625
- m_io: float32 [1024, 944], P(('dp', 'fsdp')), may hold values from -0.00390625 to 0.00390625
- m_small: float32 [1024, 9], P(('dp', 'fsdp')), may hold values from -0.015625 to 0.015625
- v_agg: float32 [1024, 3072], P(('dp', 'fsdp')), may hold values from 2.9932032e-08 to 4.789125e-07
- v_attn: float32 [1024, 4096], P(('dp', 'fsdp')), may hold values from 2.9932032e-08 to 4.789125e-07
- v_mlp: float32 [1024, 8192], P(('dp', 'fsdp')), may hold values from 2.9932032e-08 to 4.789125e-07
- v_io: float32 [1024, 944], P(('dp', 'fsdp')), may hold values from 2.9932032e-08 to 4.789125e-07
- v_small: float32 [1024, 9], P(('dp', 'fsdp')), may hold values from 4.789125e-07 to 7.6626e-06
Outputs:
- loss: float32 [], replicated
- grad_norm: float32 [], replicated
- new_agg: float32 [1024, 3072], P(('dp', 'fsdp'))
- new_attn: float32 [1024, 4096], P(('dp', 'fsdp'))
- new_mlp: float32 [1024, 8192], P(('dp', 'fsdp'))
- new_io: float32 [1024, 944], P(('dp', 'fsdp'))
- new_small: float32 [1024, 9], P(('dp', 'fsdp'))
- copy_agg: bfloat16 [1024, 3072], P(('dp', 'fsdp'))
- copy_attn: bfloat16 [1024, 4096], P(('dp', 'fsdp'))
- copy_mlp: bfloat16 [1024, 8192], P(('dp', 'fsdp'))
- copy_io: bfloat16 [1024, 944], P(('dp', 'fsdp'))
- copy_small: bfloat16 [1024, 9], P(('dp', 'fsdp'))
- moment_agg: float32 [1024, 3072], P(('dp', 'fsdp'))
- moment_attn: float32 [1024, 4096], P(('dp', 'fsdp'))
- moment_mlp: float32 [1024, 8192], P(('dp', 'fsdp'))
- moment_io: float32 [1024, 944], P(('dp', 'fsdp'))
- moment_small: float32 [1024, 9], P(('dp', 'fsdp'))
- square_agg: float32 [1024, 3072], P(('dp', 'fsdp'))
- square_attn: float32 [1024, 4096], P(('dp', 'fsdp'))
- square_mlp: float32 [1024, 8192], P(('dp', 'fsdp'))
- square_io: float32 [1024, 944], P(('dp', 'fsdp'))
- square_small: float32 [1024, 9], P(('dp', 'fsdp'))
Inputs may be any that keep to these rules, and one draw needn't show every extreme that they name: `present_vars`: every row has at least one present variable.
All inputs are finite; a program needn't handle non-finite values. No bound on the sum of `valid_mask` on one device may be relied on, other than what follows from the above.
Results may differ from a plain program's by a relative error of at most 0.0019.
The roundings to bfloat16 on the way count: a program that leaves them out, or rounds other values in their place, can miss the bound.
Values may be sent and summed in bfloat16 or wider, within the bound.
A program may use at most 384 MiB of HBM per device.

v0:
```python
import jax
import jax.numpy as jnp
from jax import lax
from jax.sharding import PartitionSpec as P

D = 1024
HEADS = 16
HEAD_DIM = 64
FF = 4096
VARS = 48
PIX = 4
LEAD_STEPS = 8
WIDTH = VARS * PIX
SPAN = 256
MIX = WIDTH + VARS
USED = 2 * WIDTH + VARS + SPAN
norm_eps = 1e-05
clip_limit = 1.0
decay_rate = 0.05
adam_eps = 1e-08
learn_rates = (0.03, 0.03, 0.03, 0.2, 0.3)
f32 = jnp.float32
bf16 = jnp.bfloat16
highest = lax.Precision.HIGHEST


def dot(left, right, dims):
    return lax.dot_general(left, right, (dims, ((), ())), preferred_element_type=f32)


def mm(left, right):
    return dot(left, right, ((1,), (0,)))


def mm_t(left, right):
    return dot(left, right, ((1,), (1,)))


def t_mm(left, right):
    return dot(left, right, ((0,), (0,)))


def exact(eq, left, right):
    return jnp.einsum(eq, left, right, precision=highest, preferred_element_type=f32)


def norm_forward(values, gain, offset):
    average = jnp.mean(values, axis=-1, keepdims=True)
    centred = values - average
    scale = lax.rsqrt(jnp.mean(centred * centred, axis=-1, keepdims=True) + norm_eps)
    unit = centred * scale
    return ((unit * gain[None] + offset[None]).astype(bf16), unit, scale)


def norm_backward(grad, unit, scale, gain):
    inner = grad * gain[None]
    mean_inner = jnp.mean(inner, axis=-1, keepdims=True)
    mean_product = jnp.mean(inner * unit, axis=-1, keepdims=True)
    back = scale * (inner - mean_inner - unit * mean_product)
    return (back, jnp.sum(grad * unit, axis=0), jnp.sum(grad, axis=0))


def adamw(weight, grad, moment, second, step_value, learn_rate):
    moment = 0.5 * moment + 0.5 * grad
    second = 0.5 * second + 0.5 * grad * grad
    correct = 1.0 - jnp.power(f32(0.5), step_value)
    update = moment / correct / (jnp.sqrt(second / correct) + adam_eps) + decay_rate * weight
    fresh = weight - learn_rate * update
    return (fresh, fresh.astype(bf16), moment, second)


def ag(part):
    return lax.all_gather(part, "fsdp", axis=0, tiled=True)


def make_local(n_dp, n_f):

    def local(
        pixels,
        targets,
        valid_mask,
        lat_weight,
        segment_ids,
        present_vars,
        lead_index,
        step_count,
        w_agg,
        w_attn,
        w_mlp,
        w_io,
        w_small,
        m_agg,
        m_attn,
        m_mlp,
        m_io,
        m_small,
        v_agg,
        v_attn,
        v_mlp,
        v_io,
        v_small,
    ):
        masters = (w_agg, w_attn, w_mlp, w_io, w_small)
        firsts = (m_agg, m_attn, m_mlp, m_io, m_small)
        seconds = (v_agg, v_attn, v_mlp, v_io, v_small)
        rows = pixels.shape[1]
        row_len = segment_ids.shape[1]
        strip = w_agg.shape[0]
        own = lax.axis_index("fsdp")
        heads_here = HEADS // n_f
        wide = heads_here * HEAD_DIM
        seg = segment_ids[0]
        seg_own = lax.dynamic_slice_in_dim(seg, own * rows, rows)
        below = jnp.sum((seg[None, :] < seg_own[:, None]).astype(jnp.int32), axis=1)
        pos = own * rows + jnp.arange(rows, dtype=jnp.int32) - below
        onehot = (pos[:, None] == jnp.arange(SPAN, dtype=jnp.int32)[None, :]).astype(bf16)
        lead = (lead_index[0].astype(f32) + 1.0) / LEAD_STEPS
        pixel_rows = pixels[0]
        target = targets[0].astype(f32)
        present = present_vars[0]
        spread = (jnp.arange(MIX) // PIX)[None, :] == jnp.arange(VARS)[:, None]
        embed_col = (jnp.arange(MIX) - WIDTH)[None, :] == jnp.arange(VARS)[:, None]
        in_pixels = (jnp.arange(MIX) < WIDTH)[None, :]
        expand = jnp.where(in_pixels, spread, embed_col).astype(bf16)
        present_cols = jnp.repeat(present.astype(f32), PIX)
        pixel_weight = lat_weight[0][:, None] * valid_mask[0].astype(f32) * present_cols[None, :]
        total = lax.psum(jnp.sum(pixel_weight), ("dp", "fsdp"))
        pack = jnp.concatenate(
            [
                w_io[:, :USED].astype(bf16),
                w_small.astype(bf16),
                jnp.zeros((strip, 768 - USED - 9), bf16),
                w_agg.astype(bf16),
            ],
            axis=1,
        )
        head = lax.all_gather(pack, ("dp", "fsdp"), axis=0, tiled=True)
        attn = lax.all_gather(w_attn.astype(bf16), ("dp", "fsdp"), axis=0, tiled=True)
        mlp = lax.all_gather(w_mlp.astype(bf16), ("dp", "fsdp"), axis=0, tiled=True)
        w240 = jnp.concatenate([head[:, :WIDTH], head[:, 2 * WIDTH : 2 * WIDTH + VARS]], axis=1)
        w_pred = head[:, WIDTH : 2 * WIDTH]
        w_pos = head[:, 2 * WIDTH + VARS : USED]
        small = head[:, USED : USED + 9].astype(f32).T
        agg_kv = head[:, 768 : 768 + 2 * D]
        agg_out = head[:, 768 + 2 * D :]
        w_qkv = attn[:, : 3 * D]
        w_out = attn[:, 3 * D :]
        w_up = mlp[:, :FF]
        w_down = mlp[:, FF:]
        pix_t = jnp.concatenate([pixel_rows.T, jnp.ones((VARS, rows), bf16)], axis=0)
        table = t_mm(w240, agg_kv)
        table_k = table[:, :D].reshape(MIX, HEADS, HEAD_DIM)
        table_v = table[:, D:].reshape(MIX, HEADS, HEAD_DIM)
        query = small[0].reshape(HEADS, HEAD_DIM)
        folded = jnp.sum(table_k * query[None], axis=2)
        block = folded.T[:, None, :] * expand.astype(f32)[None]
        score = exact("xc,cl->xl", block.reshape(HEADS * VARS, MIX), pix_t.astype(f32))
        score = score.reshape(HEADS, VARS, rows) * HEAD_DIM ** (-0.5)
        score = jnp.where(present[None, :, None] > 0, score, -1000000000.0)
        top = jnp.max(score, axis=1, keepdims=True)
        power = jnp.exp(score - top)
        soft = power / jnp.sum(power, axis=1, keepdims=True)
        share = soft.astype(bf16)
        pix_f = pix_t.astype(f32)
        lifted_share = (
            jnp.einsum("vc,hvl->hcl", expand, share, preferred_element_type=f32) * pix_f[None]
        )
        mixed_a = exact("che,hcl->hel", table_v, lifted_share).reshape(D, rows).T.astype(bf16)
        lead_embed = lead * small[7] + small[8]
        h0 = mm(mixed_a, agg_out) + mm_t(onehot, w_pos) + lead_embed[None]
        norm0, unit0, scale0 = norm_forward(h0, small[1], small[2])
        qkv = mm(norm0, w_qkv).astype(bf16)
        part = qkv.reshape(rows, 3, n_f, wide)
        part = lax.all_to_all(part, "fsdp", split_axis=2, concat_axis=0, tiled=True)
        part = part.reshape(row_len, 3, heads_here, HEAD_DIM)
        q, k, v = (part[:, i].transpose(1, 0, 2) for i in range(3))
        att_score = jnp.einsum("hqe,hke->hqk", q, k, preferred_element_type=f32) * HEAD_DIM ** (
            -0.5
        )
        same = seg[:, None] == seg[None, :]
        att_score = jnp.where(same[None], att_score, -1000000000.0)
        att_top = jnp.max(att_score, axis=-1, keepdims=True)
        att_power = jnp.exp(att_score - att_top)
        att_soft = att_power / jnp.sum(att_power, axis=-1, keepdims=True)
        att = att_soft.astype(bf16)
        mixed_h = jnp.einsum("hqk,hke->qhe", att, v, preferred_element_type=f32)
        mixed_h = mixed_h.reshape(row_len, wide).astype(bf16)
        mixed_all = lax.all_gather(mixed_h, "fsdp", axis=1, tiled=True)
        mixed = lax.dynamic_slice_in_dim(mixed_all, own * rows, rows, axis=0)
        h1 = h0 + mm(mixed, w_out)
        norm1, unit1, scale1 = norm_forward(h1, small[3], small[4])
        up = mm(norm1, w_up)
        gate = 0.5 * (1.0 + lax.erf(up * 2.0 ** (-0.5)))
        lifted = (up * gate).astype(bf16)
        h2 = h1 + mm_t(lifted, w_down)
        norm2, unit2, scale2 = norm_forward(h2, small[5], small[6])
        predicted = mm(norm2, w_pred) * D ** (-0.5)
        error = predicted - target
        weighted = pixel_weight * error
        numerator = lax.psum(jnp.sum(weighted * error), ("dp", "fsdp"))
        d_pred = (weighted * (2.0 * D ** (-0.5) / total)).astype(bf16)
        d_norm2 = mm_t(d_pred, w_pred)
        d_h2, d_gain2, d_off2 = norm_backward(d_norm2, unit2, scale2, small[5])
        d_out = d_h2.astype(bf16)
        slope = gate + up * jnp.exp(-0.5 * up * up) * 0.3989422804014327
        d_up = (mm(d_out, w_down) * slope).astype(bf16)
        d_norm1 = mm_t(d_up, w_up)
        d_in, d_gain1, d_off1 = norm_backward(d_norm1, unit1, scale1, small[3])
        d_h1 = d_h2 + d_in
        d_proj_all = ag(d_h1.astype(bf16))
        w_out_own = lax.dynamic_slice_in_dim(w_out, own * wide, wide, axis=0)
        d_mixed = (
            mm_t(d_proj_all, w_out_own)
            .astype(bf16)
            .reshape(row_len, heads_here, HEAD_DIM)
            .transpose(1, 0, 2)
        )
        d_att = jnp.einsum("hqe,hke->hqk", d_mixed, v, preferred_element_type=f32)
        d_v = jnp.einsum("hqk,hqe->khe", att, d_mixed, preferred_element_type=f32)
        lean = jnp.sum(att_soft * d_att, axis=-1, keepdims=True)
        d_score = (att_soft * (d_att - lean) * HEAD_DIM ** (-0.5)).astype(bf16)
        d_q = jnp.einsum("hqk,hke->qhe", d_score, k, preferred_element_type=f32)
        d_k = jnp.einsum("hqk,hqe->khe", d_score, q, preferred_element_type=f32)
        d_part = jnp.stack([d_q, d_k, d_v], axis=1).astype(bf16).reshape(row_len, 3, 1, wide)
        d_qkv_all = lax.all_gather(d_part, "fsdp", axis=2, tiled=True).reshape(row_len, 3 * D)
        d_qkv = lax.dynamic_slice_in_dim(d_qkv_all, own * rows, rows, axis=0)
        d_norm0 = mm_t(d_qkv, w_qkv)
        d_in, d_gain0, d_off0 = norm_backward(d_norm0, unit0, scale0, small[1])
        d_h0 = d_h1 + d_in
        d_agg = d_h0.astype(bf16)
        d_mixed_a = mm_t(agg_out, d_agg).astype(bf16).reshape(HEADS, HEAD_DIM, rows)
        pulled = exact("che,hel->hcl", table_v, d_mixed_a.astype(f32)) * pix_f[None]
        d_share = exact("vc,hcl->hvl", expand.astype(f32), pulled)
        lean_a = jnp.sum(soft * d_share, axis=1, keepdims=True)
        d_score_a = (soft * (d_share - lean_a) * HEAD_DIM ** (-0.5)).astype(bf16)
        spread_score = jnp.einsum("vc,hvl->hcl", expand, d_score_a, preferred_element_type=f32)
        d_folded = jnp.sum(spread_score * pix_f[None], axis=2)
        d_table_v = exact("hcl,hel->che", lifted_share, d_mixed_a.astype(f32)).reshape(MIX, D)
        d_table_k = (d_folded.T[:, :, None] * query[None]).reshape(MIX, D)
        d_query = jnp.sum(d_folded.T[:, :, None] * table_k, axis=0).reshape(D)
        d_bias = jnp.sum(d_h0, axis=0)
        narrow = jnp.stack(
            [d_query, d_gain0, d_off0, d_gain1, d_off1, d_gain2, d_off2, lead * d_bias, d_bias]
            + [jnp.zeros((D,), f32)] * 7
        )
        d_table, narrow = lax.psum(
            (jnp.concatenate([d_table_k, d_table_v], axis=1), narrow), "fsdp"
        )

        def mine(array):
            whole = array.reshape(n_dp, n_f, strip, array.shape[1])
            return lax.dynamic_index_in_dim(whole, own, axis=1, keepdims=False).reshape(
                n_dp * strip, array.shape[1]
            )

        source = jnp.arange(D)
        pick = source // strip % n_f == own
        place = source // (strip * n_f) * strip + source % strip
        choose = (pick[:, None] & (place[:, None] == jnp.arange(n_dp * strip)[None, :])).astype(
            bf16
        )

        def weight_grad(features, grads):
            return t_mm(mm(features, choose).astype(bf16), grads)

        d_agg_all = ag(d_agg)
        g_attn = jnp.concatenate(
            [weight_grad(ag(norm0), d_qkv_all), weight_grad(mixed_all, d_proj_all)], axis=1
        )
        g_mlp = jnp.concatenate(
            [weight_grad(ag(norm1), ag(d_up)), weight_grad(ag(d_out), ag(lifted))], axis=1
        )
        g_out = weight_grad(ag(mixed_a), d_agg_all)
        g_kv = exact("dc,cx->dx", mine(w240).astype(f32), d_table)
        g_240 = exact("dx,cx->dc", mine(agg_kv).astype(f32), d_table)
        g_pred = weight_grad(ag(norm2), ag(d_pred))
        g_pos = weight_grad(d_agg_all, ag(onehot))
        g_small = mine(narrow.T)[:, :9]
        g_agg = jnp.concatenate([g_kv, g_out], axis=1)
        g_misc = jnp.concatenate(
            [
                g_240[:, :WIDTH],
                g_pred,
                g_240[:, WIDTH:],
                g_pos,
                g_small,
                jnp.zeros((n_dp * strip, 768 - USED - 9), f32),
            ],
            axis=1,
        )
        r_agg, r_attn, r_mlp, r_misc = (
            lax.psum_scatter(g, "dp", scatter_dimension=0, tiled=True)
            for g in (g_agg, g_attn, g_mlp, g_misc)
        )
        r_io = jnp.concatenate(
            [r_misc[:, :USED], jnp.zeros((strip, w_io.shape[1] - USED), f32)], axis=1
        )
        reduced = (r_agg, r_attn, r_mlp, r_io, r_misc[:, USED : USED + 9])
        squares = lax.psum(sum((jnp.sum(piece * piece) for piece in reduced)), ("dp", "fsdp"))
        grad_norm = jnp.sqrt(squares)
        factor = jnp.minimum(1.0, clip_limit / grad_norm)
        loss = numerator / total
        step_value = step_count[0].astype(f32)
        results = [
            adamw(
                masters[i], reduced[i] * factor, firsts[i], seconds[i], step_value, learn_rates[i]
            )
            for i in range(5)
        ]
        return (loss, grad_norm) + tuple((results[i][j] for j in range(4) for i in range(5)))

    return local


def solution(mesh):
    flat = P(("dp", "fsdp"), None)
    tokens = P("dp", "fsdp", None)
    return jax.shard_map(
        make_local(mesh.shape["dp"], mesh.shape["fsdp"]),
        mesh=mesh,
        in_specs=(
            tokens,
            tokens,
            tokens,
            P("dp", "fsdp"),
            P("dp", None),
            P("dp", None),
            P("dp"),
            P(),
        )
        + (flat,) * 15,
        out_specs=(P(), P()) + (flat,) * 20,
        check_vma=False,
    )
```

profile of v0, /device:TPU:0, one launch (start us, length us, event | category | flops | bytes accessed | tf_op | source)
XLA Modules:
  0.0 1196.0 jit_solution(15080212584497687655)
XLA Ops:
  16.4 73.1 %all-gather.15.cloned.1.call-done = bf16[1024,3840]{1,0:T(8,128)(2,1)} async-done(((bf16[32,3840]{1,0:T(8,128)(2,1)}), bf16[1024,3840]{1,0:T(8,128)(2,1)}) %all-gather.15.cloned.1.call-update) | async-done | bytes 7864336 | tf_op jit(solution)/shard_map/all_gather | solution.py:137
  93.0 3.6 fusion.204
  102.4 2.3 fusion.114
  105.9 2.3 fusion.77
  108.9 2.3 fusion.222
  112.8 56.2 %all-gather.17.cloned.1.call-done = bf16[1024,4096]{1,0:T(8,128)(2,1)} async-done(((bf16[32,4096]{1,0:T(8,128)(2,1)}), bf16[1024,4096]{1,0:T(8,128)(2,1)}) %all-gather.17.cloned.1.call-update) | async-done | bytes 8388624 | tf_op jit(solution)/shard_map/all_gather | solution.py:138
  169.0 4.8 fusion.23
  173.8 2.6 reshape.422
  176.4 2.1 copy.178
  178.5 4.2 all-to-all-start
  184.0 10.5 all-to-all-done
  194.5 2.2 copy.179
  196.7 2.3 reshape.423
  199.0 5.3 fusion.223
  204.4 3.4 convolution_convert_fusion.9
  212.7 10.5 all-gather.19.cloned.1.call-done
  223.3 2.2 fusion.224
  227.2 114.3 %all-gather.21.cloned.1.call-done = bf16[1024,8192]{1,0:T(8,128)(2,1)} async-done(((bf16[32,8192]{1,0:T(8,128)(2,1)}), bf16[1024,8192]{1,0:T(8,128)(2,1)}) %all-gather.21.cloned.1.call-update) | async-done | bytes 16777232 | tf_op jit(solution)/shard_map/all_gather | solution.py:139
  341.4 6.7 multiply_convert_fusion.1
  348.1 6.7 fusion.225
  356.6 3.2 fusion.165
  359.7 39.0 %psum.36 = f32[]{:T(128)} all-reduce(f32[]{:T(128)} %get-tuple-element.166), channel_id=1, replica_groups=mesh['dp'=8,'fsdp'=4] {'dp','fsdp'}, use_global_device_ids=true, to_apply=%region_15.16 | all-reduce | flops 1 | bytes 8 | tf_op jit(solution)/shard_map/psum | solution.py:127
  400.5 2.5 multiply_reduce_fusion.4
  402.9 2.2 fusion.218
  405.1 7.0 fusion.19
  412.2 7.5 multiply_reduce_fusion.5
  420.9 3.1 slice.146
  424.0 14.7 %all-gather.23.cloned.1.call-done = bf16[512,1024]{1,0:T(8,128)(2,1)} async-done(((bf16[128,1024]{1,0:T(8,128)(2,1)}), bf16[512,1024]{1,0:T(8,128)(2,1)}) %all-gather.23.cloned.1.call-update) | async-done | bytes 1048592 | tf_op jit(solution)/shard_map/all_gather | solution.py:73
  440.5 3.7 convolution_convert_fusion.7
  444.2 3.6 fusion.156
  447.8 8.1 fusion.73
  456.0 8.5 fusion.70
  467.5 27.7 %all-gather.25.cloned.1.call-done = bf16[512,3,4,256]{0,3,2,1:T(8,128)(2,1)} async-done(((bf16[512,3,1,256]{0,3,2,1:T(8,128)(2,1)}), bf16[512,3,4,256]{0,3,2,1:T(8,128)(2,1)}) %all-gather.25.cloned.1.call-update) | async-done | bytes 3145744 | tf_op jit(solution)/shard_map/all_gather | solution.py:225
  495.2 6.1 multiply_reduce_fusion.6
  502.3 2.4 fusion.67
  523.0 7.3 all_gather.63
  530.4 2.2 slice-done
  532.7 7.9 all_gather.62
  542.6 34.1 %all-reduce.6.cloned.1.call-done = (f32[240,2048]{0,1:T(8,128)}, f32[8,4,32,16]{2,1,0,3:T(4,128)}) async-done(((f32[240,2048]{0,1:T(8,128)}, f32[8,4,32,16]{2,1,0,3:T(4,128)}), (f32[240,2048]{0,1:T(8,128)}, f32[8,4,32,16]{2,1,0,3:T(4,128)})) %all-reduce.6.cloned.1.call-update) | async-done | bytes 2031632 | tf_op jit(solution)/shard_map/psum | solution.py:246
  576.7 3.4 fusion.228
  581.4 14.3 %all-gather.29.cloned.1.call-done = bf16[512,1024]{1,0:T(8,128)(2,1)} async-done(((bf16[128,1024]{1,0:T(8,128)(2,1)}), bf16[512,1024]{1,0:T(8,128)(2,1)}) %all-gather.29.cloned.1.call-update) | async-done | bytes 1048592 | tf_op jit(solution)/shard_map/all_gather | solution.py:73
  600.2 2.8 fusion.227
  603.0 10.9 all-gather.27.cloned.1.call-done
  614.0 3.0 fusion.82
  619.0 4.0 fusion.83
  623.0 10.0 all-gather.31.cloned.1.call-done
  632.9 4.2 fusion.84
  637.1 3.5 pad_maximum_fusion.1
  641.0 10.7 all-gather.37.cloned.1.call-done
  651.7 36.7 %all-gather.39.cloned.1.call-done = bf16[512,4096]{1,0:T(8,128)(2,1)} async-done(((bf16[128,4096]{1,0:T(8,128)(2,1)}), bf16[512,4096]{1,0:T(8,128)(2,1)}) %all-gather.39.cloned.1.call-update) | async-done | bytes 4194320 | tf_op jit(solution)/shard_map/all_gather | solution.py:73
  688.3 6.7 fusion.86
  695.1 12.0 %all-gather.33.cloned.1.call-done = bf16[512,1024]{1,0:T(8,128)(2,1)} async-done(((bf16[128,1024]{1,0:T(8,128)(2,1)}), bf16[512,1024]{1,0:T(8,128)(2,1)}) %all-gather.33.cloned.1.call-update) | async-done | bytes 1048592 | tf_op jit(solution)/shard_map/all_gather | solution.py:73
  707.1 36.5 %all-gather.35.cloned.1.call-done = bf16[512,4096]{1,0:T(8,128)(2,1)} async-done(((bf16[128,4096]{1,0:T(8,128)(2,1)}), bf16[512,4096]{1,0:T(8,128)(2,1)}) %all-gather.35.cloned.1.call-update) | async-done | bytes 4194320 | tf_op jit(solution)/shard_map/all_gather | solution.py:73
  743.6 6.7 fusion.85
  750.3 7.6 pad_maximum_fusion
  758.7 50.6 %reduce-scatter.13.cloned.1.call-done = f32[32,768]{1,0:T(8,128)} async-done(((f32[256,768]{1,0:T(8,128)}), f32[32,768]{1,0:T(8,128)}) %reduce-scatter.13.cloned.1.call-update) | async-done | bytes 98320 | tf_op jit(solution)/shard_map/reduce_scatter | solution.py:292
  812.3 74.4 %reduce-scatter.7.cloned.1.call-done = f32[32,3072]{1,0:T(8,128)} async-done(((f32[256,3072]{1,0:T(8,128)}), f32[32,3072]{1,0:T(8,128)}) %reduce-scatter.7.cloned.1.call-update) | async-done | bytes 393232 | tf_op jit(solution)/shard_map/reduce_scatter | solution.py:292
  888.3 89.3 %reduce-scatter.9.cloned.1.call-done = f32[32,4096]{1,0:T(8,128)} async-done(((f32[256,4096]{1,0:T(8,128)}), f32[32,4096]{1,0:T(8,128)}) %reduce-scatter.9.cloned.1.call-update) | async-done | bytes 524304 | tf_op jit(solution)/shard_map/reduce_scatter | solution.py:292
  980.8 149.3 %reduce-scatter.11.cloned.1.call-done = f32[32,8192]{1,0:T(8,128)} async-done(((f32[256,8192]{1,0:T(8,128)}), f32[32,8192]{1,0:T(8,128)}) %reduce-scatter.11.cloned.1.call-update) | async-done | bytes 1048592 | tf_op jit(solution)/shard_map/reduce_scatter | solution.py:292
  1130.0 2.1 multiply_reduce_fusion.1
  1134.2 39.4 %all-reduce.2 = (f32[]{:T(128)}, f32[]{:T(128)}) all-reduce(f32[]{:T(128)} %get-tuple-element.167, f32[]{:T(128)S(6)} %add.312), channel_id=1, replica_groups=mesh['dp'=8,'fsdp'=4] {'dp','fsdp'}, use_global_device_ids=true, to_apply=%region_13.14 | all-reduce | flops 2 | bytes 16 | tf_op jit(solution)/shard_map/psum | solution.py:200
  1179.1 2.5 fusion.214
  1181.6 2.7 fusion.212
  1184.3 2.5 fusion.210
  (248 shorter events, 76.6 us)
Async XLA Ops:
  7.2 82.3 %all-gather.15.cloned.1.call-start = ((), (), s32[]{:S(2)}) async-start(), calls=%async_computation.5 | async-start | bytes 8110080 | tf_op jit(solution)/shard_map/all_gather | solution.py:137
  10.8 158.2 %all-gather.17.cloned.1.call-start = ((), (), s32[]{:S(2)}) async-start(), calls=%async_computation.6 | async-start | bytes 8650752 | tf_op jit(solution)/shard_map/all_gather | solution.py:138
  13.3 79.7 %copy-start.37 = (pred[240]{0:T(512)(128)(4,1)}, pred[240]{0:T(512)(128)(4,1)S(1)}, u32[]{:S(2)}) copy-start(pred[240]{0:T(512)(128)(4,1)S(1)} %iota_compare_fusion.5) | copy-start | bytes 724
  14.0 79.0 %copy-start.28 = (s32[240]{0:T(256)}, s32[240]{0:T(256)S(1)}, u32[]{:S(2)}) copy-start(s32[240]{0:T(256)S(1)} %get-tuple-element.225) | copy-start | bytes 2884
  14.0 79.0 %copy-start.30 = (s32[240]{0:T(256)}, s32[240]{0:T(256)S(1)}, u32[]{:S(2)}) copy-start(s32[240]{0:T(256)S(1)} %get-tuple-element.226) | copy-start | bytes 2884
  14.8 91.1 %copy-start.12 = (f32[240,128]{1,0:T(8,128)}, f32[240,128]{1,0:T(8,128)S(1)}, u32[]{:S(2)}) copy-start(f32[240,128]{1,0:T(8,128)S(1)} %pad_convert_fusion) | copy-start | bytes 368644
  15.7 86.7 %copy-start.47 = (s32[128]{0:T(128)}, s32[128]{0:T(128)S(1)}, u32[]{:S(2)}) copy-start(s32[128]{0:T(128)S(1)} %add_subtract_fusion) | copy-start | bytes 1540
  93.0 4.8 copy-start.17
  96.6 4.4 copy-start.20
  102.4 5.8 copy-start.21
  173.8 9.3 copy-start.24
  178.5 15.9 %all-to-all-start = ((bf16[128,3,4,256]{3,0,1,2:T(8,128)(2,1)}), bf16[128,3,4,256]{3,0,1,2:T(8,128)(2,1)}, u32[]{:S(2)}, u32[]{:S(2)}) async-start(bf16[128,3,4,256]{3,0,1,2:T(8,128)(2,1)} %copy.178), calls=%async_computation | async-start | bytes 1572864 | tf_op jit(solution)/shard_map/all_to_all | solution.py:174
  182.8 40.5 %all-gather.19.cloned.1.call-start = ((), (), s32[]{:S(2)}) async-start(), calls=%async_computation.7 | async-start | bytes 1310720 | tf_op jit(solution)/shard_map/all_gather | solution.py:188
  207.8 18.5 %copy-start.27 = (f32[1,1024]{1,0:T(1,128)S(1)}, f32[1,1024]{1,0:T(1,128)}, u32[]{:S(2)}) copy-start(f32[1,1024]{1,0:T(1,128)} %get-tuple-element.203) | copy-start | bytes 12292
  207.8 133.6 %all-gather.21.cloned.1.call-start = ((), (), s32[]{:S(2)}) async-start(), calls=%async_computation.8 | async-start | bytes 17301504 | tf_op jit(solution)/shard_map/all_gather | solution.py:139
  209.9 228.7 %all-gather.23.cloned.1.call-start = ((), (), s32[]{:S(2)}) async-start(), calls=%async_computation.9 | async-start | bytes 1310720 | tf_op jit(solution)/shard_map/all_gather | solution.py:73
  348.1 7.5 copy-start.26
  348.1 8.4 copy-start.32
  400.4 4.7 copy-start.18
  405.1 7.1 copy-start.40
  405.1 7.1 copy-start.54
  412.2 7.5 copy-start.1
  412.2 7.5 copy-start.11
  420.8 19.7 %copy-start.55 = (f32[4,512]{1,0:T(4,128)S(1)}, f32[4,512]{1,0:T(4,128)}, u32[]{:S(2)}) copy-start(f32[4,512]{1,0:T(4,128)} %get-tuple-element.213) | copy-start | bytes 24580
  420.8 74.4 %all-gather.25.cloned.1.call-start = ((), (), s32[]{:S(2)}) async-start(), calls=%async_computation.10 | async-start | bytes 3932160 | tf_op jit(solution)/shard_map/all_gather | solution.py:225
  455.9 39.3 %copy-start.34 = (f32[128]{0:T(128)S(1)}, f32[128]{0:T(128)}, u32[]{:S(2)}) copy-start(f32[128]{0:T(128)} %copy-done.33) | copy-start | bytes 1540
  455.9 39.3 %copy-start.50 = (f32[128]{0:T(128)S(1)}, f32[128]{0:T(128)}, u32[]{:S(2)}) copy-start(f32[128]{0:T(128)} %copy-done.49) | copy-start | bytes 1540
  466.5 74.1 %all-gather.41.cloned.1.call-start = ((), (), s32[]{:S(2)}) async-start(), calls=%async_computation.21 | async-start | bytes 1310720 | tf_op jit(solution)/shard_map/all_gather | solution.py:73
  467.3 109.5 %all-reduce.6.cloned.1.call-start = ((), (), s32[]{:S(2)}) async-start(), calls=%async_computation.23 | async-start | bytes 4718592 | tf_op jit(solution)/shard_map/psum | solution.py:246
  495.2 6.1 copy-start.10
  495.2 6.1 copy-start.35
  495.2 6.1 copy-start.51
  501.3 5.2 copy-start.29
  501.3 5.2 copy-start.31
  502.3 4.3 copy-start.38
  502.3 5.2 copy-start.22
  504.7 4.9 copy-start.25
  507.5 6.4 copy-start.41
  507.5 6.4 copy-start.42
  507.5 6.3 copy-start.43
  507.5 6.3 copy-start.44
  507.5 6.3 copy-start.45
  507.6 6.3 copy-start.46
  512.1 4.7 copy-start.6
  516.8 6.1 copy-start.48
  518.3 77.4 %all-gather.29.cloned.1.call-start = ((), (), s32[]{:S(2)}) async-start(), calls=%async_computation.12 | async-start | bytes 1310720 | tf_op jit(solution)/shard_map/all_gather | solution.py:73
  519.0 94.9 %all-gather.27.cloned.1.call-start = ((), (), s32[]{:S(2)}) async-start(), calls=%async_computation.11 | async-start | bytes 1310720 | tf_op jit(solution)/shard_map/all_gather | solution.py:73
  519.6 113.3 %all-gather.31.cloned.1.call-start = ((), (), s32[]{:S(2)}) async-start(), calls=%async_computation.14 | async-start | bytes 1310720 | tf_op jit(solution)/shard_map/all_gather | solution.py:73
  520.4 131.3 %all-gather.37.cloned.1.call-start = ((), (), s32[]{:S(2)}) async-start(), calls=%async_computation.18 | async-start | bytes 1310720 | tf_op jit(solution)/shard_map/all_gather | solution.py:73
  520.9 167.4 %all-gather.39.cloned.1.call-start = ((), (), s32[]{:S(2)}) async-start(), calls=%async_computation.19 | async-start | bytes 5242880 | tf_op jit(solution)/shard_map/all_gather | solution.py:73
  521.7 185.4 %all-gather.33.cloned.1.call-start = ((), (), s32[]{:S(2)}) async-start(), calls=%async_computation.16 | async-start | bytes 1310720 | tf_op jit(solution)/shard_map/all_gather | solution.py:73
  522.3 221.3 %all-gather.35.cloned.1.call-start = ((), (), s32[]{:S(2)}) async-start(), calls=%async_computation.17 | async-start | bytes 5242880 | tf_op jit(solution)/shard_map/all_gather | solution.py:73
  522.9 286.4 %reduce-scatter.13.cloned.1.call-start = ((), (), s32[]{:S(2)}) async-start(), calls=%async_computation.22 | async-start | bytes 884736 | tf_op jit(solution)/shard_map/reduce_scatter | solution.py:292
  599.2 287.4 %reduce-scatter.7.cloned.1.call-start = ((), (), s32[]{:S(2)}) async-start(), calls=%async_computation.13 | async-start | bytes 3538944 | tf_op jit(solution)/shard_map/reduce_scatter | solution.py:292
  618.9 358.7 %reduce-scatter.9.cloned.1.call-start = ((), (), s32[]{:S(2)}) async-start(), calls=%async_computation.15 | async-start | bytes 4718592 | tf_op jit(solution)/shard_map/reduce_scatter | solution.py:292
  640.6 489.4 %reduce-scatter.11.cloned.1.call-start = ((), (), s32[]{:S(2)}) async-start(), calls=%async_computation.20 | async-start | bytes 9437184 | tf_op jit(solution)/shard_map/reduce_scatter | solution.py:292
  757.9 419.8 %copy-start.23 = (f32[32,9]{0,1:T(8,128)S(1)}, f32[32,9]{0,1:T(8,128)}, u32[]{:S(2)}) copy-start(f32[32,9]{0,1:T(8,128)} %param.35) | copy-start | bytes 3460
  757.9 421.2 %copy-start.14 = (f32[32,3072]{1,0:T(8,128)S(1)}, f32[32,3072]{1,0:T(8,128)}, u32[]{:S(2)}) copy-start(f32[32,3072]{1,0:T(8,128)} %param.31) | copy-start | bytes 1179652
  757.9 423.7 %copy-start.8 = (f32[32,4096]{1,0:T(8,128)S(1)}, f32[32,4096]{1,0:T(8,128)}, u32[]{:S(2)}) copy-start(f32[32,4096]{1,0:T(8,128)} %param.32) | copy-start | bytes 1572868
  977.6 204.0 %copy-start.9 = (f32[32,4096]{1,0:T(8,128)S(1)}, f32[32,4096]{1,0:T(8,128)}, u32[]{:S(2)}) copy-start(f32[32,4096]{1,0:T(8,128)} %reduce-scatter.9.cloned.1.call-done) | copy-start | bytes 1572868
  1132.1 52.2 %copy-start.4 = (f32[32,8192]{1,0:T(8,128)S(1)}, f32[32,8192]{1,0:T(8,128)}, u32[]{:S(2)}) copy-start(f32[32,8192]{1,0:T(8,128)} %param.33) | copy-start | bytes 3145732
  1132.1 52.2 %copy-start.5 = (f32[32,8192]{1,0:T(8,128)S(1)}, f32[32,8192]{1,0:T(8,128)}, u32[]{:S(2)}) copy-start(f32[32,8192]{1,0:T(8,128)} %reduce-scatter.11.cloned.1.call-done) | copy-start | bytes 3145732
  1175.7 8.6 copy-start.15
  1175.7 8.6 copy-start.16
  (13 other events, 16.5 us)
Sparse Core Ops, SparseCore 0:
  11.5 77.9 all-gather.14
  92.9 76.0 all-gather.16
  207.9 15.2 all-gather.18
  226.5 114.8 all-gather.20
  420.9 17.6 all-gather.22
  466.6 28.5 all-gather.24
  497.3 16.7 all-gather.40
  518.4 58.2 all-reduce.5
  578.9 16.7 all-gather.28
  597.1 16.8 all-gather.26
  616.1 16.7 all-gather.30
  634.9 16.7 all-gather.36
  653.8 34.4 all-gather.38
  690.3 16.7 all-gather.32
  709.1 34.4 all-gather.34
  746.7 62.4 reduce-scatter.12
  813.1 73.4 reduce-scatter.6
  890.6 87.0 reduce-scatter.8
  981.2 148.7 reduce-scatter.10
where the time goes:
time: 1200 us
  waiting for transfers between devices  841 us (70%)
  matrix products  137 us (11%)
  blocking collectives  93.6 us (8%)
  other arithmetic  58.3 us (5%)
  local copies, waits for them, and re-layouts  35.5 us (3%)
  between operations  25.1 us (2%)
    reduce_scatter x4, waiting for transfers between devices, local(): lax.psum_scatter(g, 'dp', scatter_dimension=0, tiled=True)  363 us
    all_gather x9, waiting for transfers between devices, ag(): return lax.all_gather(part, 'fsdp', axis=0, tiled=True)  146 us
    all_gather x1, waiting for transfers between devices, local(): mlp = lax.all_gather(w_mlp.astype(bf16), ('dp', 'fsdp'), axis=0, tiled=True)  114 us
    dot_general x21, matrix products, dot(): lax.dot_general(left, right, (dims, ((), ())), preferred_element_type=f32)  87.7 us
    all_gather x1, waiting for transfers between devices, local(): head = lax.all_gather(pack, ('dp', 'fsdp'), axis=0, tiled=True)  73.1 us
    all_gather x1, waiting for transfers between devices, local(): lax.all_gather(w_attn.astype(bf16), ('dp', 'fsdp'), axis=0, tiled=True)  56.2 us
    psum x1, blocking collectives, local(): numerator = lax.psum(jnp.sum(weighted * error), ('dp', 'fsdp'))  39.4 us
    psum x1, blocking collectives, local(): total = lax.psum(jnp.sum(pixel_weight), ('dp', 'fsdp'))  39 us
  transfers between devices with their start and end apart: 20, of which 19 were waited for; matrix products, arithmetic and copies ran while one was open for 10% of the time, Pallas kernels for 0%

commit v1 on v0

--- a/solution.py
+++ b/solution.py
@@ -24,6 +24,22 @@
 highest = lax.Precision.HIGHEST
 
 
+def ring_gather(x, axis, dim):
+    ways, here, turn = (lax.axis_size(axis), lax.axis_index(axis), x.shape[dim])
+    shape = [n * ways if d == dim else n for d, n in enumerate(x.shape)]
+    full = lax.dynamic_update_slice_in_dim(jnp.zeros(shape, x.dtype), x, here * turn, axis=dim)
+    going_up = going_down = x
+    for far in range(1, ways // 2 + 1):
+        going_up = lax.ppermute(going_up, axis, [(d, (d + 1) % ways) for d in range(ways)])
+        full = lax.dynamic_update_slice_in_dim(full, going_up, (here - far) % ways * turn, axis=dim)
+        if 2 * far < ways:
+            going_down = lax.ppermute(going_down, axis, [(d, (d - 1) % ways) for d in range(ways)])
+            full = lax.dynamic_update_slice_in_dim(
+                full, going_down, (here + far) % ways * turn, axis=dim
+            )
+    return full
+
+
 def dot(left, right, dims):
     return lax.dot_general(left, right, (dims, ((), ())), preferred_element_type=f32)
 
@@ -70,7 +86,7 @@
 
 
 def ag(part):
-    return lax.all_gather(part, "fsdp", axis=0, tiled=True)
+    return ring_gather(part, "fsdp", 0)
 
 
 def make_local(n_dp, n_f):

time: 1200 us -> 1060 us (0.88)
  waiting for transfers between devices: 841 us -> 646 us
  local copies, waits for them, and re-layouts: 35.5 us -> 80.5 us
  starting transfers between devices: 5.61 us -> 34.3 us
  blocking collectives: 93.6 us -> 78.3 us
    all_gather x9 -> x0, waiting for transfers between devices: 146 us -> none  [ag(): return lax.all_gather(part, 'fsdp', axis=0, tiled=True)]
    reduce_scatter x4, waiting for transfers between devices: 363 us -> 232 us  [local(): lax.psum_scatter(g, 'dp', scatter_dimension=0, tiled=True)]
    ppermute x0 -> x33, waiting for transfers between devices: none -> 108 us  [the longest x22 87.6 us: ring_gather(): lax.ppermute(going_up, axis, [(d, (d + 1) % ways) for d in range(ways)])]
    ppermute x0 -> x33, starting transfers between devices: none -> 29.5 us  [the longest x22 21 us: ring_gather(): lax.ppermute(going_up, axis, [(d, (d + 1) % ways) for d in range(ways)])]
    dynamic_update_slice x0 -> x35, local copies, waits for them, and re-layouts: none -> 29.3 us  [the longest x22 18.7 us: ring_gather(): lax.dynamic_update_slice_in_dim(full, going_up, (here - far) % ways * tur...]
    all_gather x1, waiting for transfers between devices: 27.7 us -> 0.02 us  [local(): lax.all_gather(d_part, 'fsdp', axis=2, tiled=True).reshape(row_len, 3 * D)]
    all_gather x2 -> x0, blocking collectives: 15.3 us -> none  [ag(): return lax.all_gather(part, 'fsdp', axis=0, tiled=True)]
  transfers between devices with their start and end apart: 20 -> 44, of which waited for: 19 -> 25; matrix products, arithmetic and copies ran while one was open for 10% -> 14% of each run, Pallas kernels for 0% -> 0%
where the time goes in v1:
time: 1060 us; the launch traced here: 1050 us
  waiting for transfers between devices  646 us (61%)
  matrix products  133 us (13%)
  local copies, waits for them, and re-layouts  80.5 us (8%)
  blocking collectives  78.3 us (7%)
  other arithmetic  56.2 us (5%)
  starting transfers between devices  34.3 us (3%)
  between operations  25.7 us (2%)
    reduce_scatter x4, waiting for transfers between devices, local(): lax.psum_scatter(g, 'dp', scatter_dimension=0, tiled=True)  232 us
    all_gather x1, waiting for transfers between devices, local(): mlp = lax.all_gather(w_mlp.astype(bf16), ('dp', 'fsdp'), axis=0, tiled=True)  114 us
    ppermute x22, waiting for transfers between devices, ring_gather(): lax.ppermute(going_up, axis, [(d, (d + 1) % ways) for d in range(ways)])  87.6 us
    dot_general x21, matrix products, dot(): lax.dot_general(left, right, (dims, ((), ())), preferred_element_type=f32)  84 us
    all_gather x1, waiting for transfers between devices, local(): head = lax.all_gather(pack, ('dp', 'fsdp'), axis=0, tiled=True)  73.1 us
    all_gather x1, waiting for transfers between devices, local(): lax.all_gather(w_attn.astype(bf16), ('dp', 'fsdp'), axis=0, tiled=True)  56.5 us
    psum x1, waiting for transfers between devices, local(): lax.psum((jnp.concatenate([d_table_k, d_table_v], axis=1), narrow), 'fsdp')  42.1 us
    psum x1, blocking collectives, local(): numerator = lax.psum(jnp.sum(weighted * error), ('dp', 'fsdp'))  39.3 us
  transfers between devices with their start and end apart: 44, of which 25 were waited for; matrix products, arithmetic and copies ran while one was open for 14% of the time, Pallas kernels for 0%

profile of v1, /device:TPU:0, one launch (start us, length us, event | category | flops | bytes accessed | tf_op | source)
XLA Modules:
  0.0 1054.2 jit_solution(1515166546633543917)
XLA Ops:
  16.4 73.1 %all-gather.6.cloned.1.call-done = bf16[1024,3840]{1,0:T(8,128)(2,1)} async-done(((bf16[32,3840]{1,0:T(8,128)(2,1)}), bf16[1024,3840]{1,0:T(8,128)(2,1)}) %all-gather.6.cloned.1.call-update) | async-done | bytes 7864336 | tf_op jit(solution)/shard_map/all_gather | solution.py:153
  91.7 3.6 fusion.205
  101.0 2.3 fusion.114
  104.9 2.3 fusion.77
  107.9 2.3 fusion.221
  112.5 56.5 %all-gather.8.cloned.1.call-done = bf16[1024,4096]{1,0:T(8,128)(2,1)} async-done(((bf16[32,4096]{1,0:T(8,128)(2,1)}), bf16[1024,4096]{1,0:T(8,128)(2,1)}) %all-gather.8.cloned.1.call-update) | async-done | bytes 8388624 | tf_op jit(solution)/shard_map/all_gather | solution.py:154
  169.0 4.8 fusion.23
  173.7 2.6 reshape.422
  178.5 4.2 all-to-all-start
  183.9 10.5 all-to-all-done
  194.4 2.2 copy.207
  196.6 2.4 reshape.423
  199.0 5.4 fusion.222
  204.4 3.4 convolution_convert_fusion.9
  212.8 10.5 all-gather.10.cloned.1.call-done
  223.3 2.2 fusion.223
  227.9 113.6 %all-gather.12.cloned.1.call-done = bf16[1024,8192]{1,0:T(8,128)(2,1)} async-done(((bf16[32,8192]{1,0:T(8,128)(2,1)}), bf16[1024,8192]{1,0:T(8,128)(2,1)}) %all-gather.12.cloned.1.call-update) | async-done | bytes 16777232 | tf_op jit(solution)/shard_map/all_gather | solution.py:155
  341.5 2.5 broadcast.380.clone
  344.0 6.8 constant_dynamic-update-slice_fusion.14
  350.8 6.8 fusion.224
  360.0 2.9 fusion.165
  362.9 39.0 %psum.36 = f32[]{:T(128)} all-reduce(f32[]{:T(128)} %get-tuple-element.166), channel_id=1, replica_groups=mesh['dp'=8,'fsdp'=4] {'dp','fsdp'}, use_global_device_ids=true, to_apply=%region_15.16 | all-reduce | flops 1 | bytes 8 | tf_op jit(solution)/shard_map/psum | solution.py:143
  404.9 2.6 multiply_reduce_fusion.4
  410.6 2.4 broadcast.380
  413.1 6.5 constant_dynamic-update-slice_fusion.22
  419.6 7.4 multiply_reduce_fusion.5
  431.0 4.6 collective-permute-done
  435.5 2.3 collective-permute-start.2
  444.3 3.7 fusion.156
  448.0 8.7 fusion.70
  456.7 8.4 fusion.73
  465.1 3.0 convolution_convert_fusion.7
  470.0 2.3 collective-permute-start.30
  474.0 2.6 collective-permute-start.32
  482.0 2.4 collective-permute-start.3
  488.9 8.2 collective-permute-done.27
  498.7 4.3 collective-permute-start.29
  503.6 6.4 collective-permute-done.29
  512.4 6.0 multiply_reduce_fusion.6
  520.5 2.3 fusion.67
  524.7 2.9 fusion.47
  527.6 2.5 collective-permute-start.6
  545.2 8.2 collective-permute-done.7
  557.4 42.1 %all-reduce.6.cloned.1.call-done = (f32[240,2048]{0,1:T(8,128)}, f32[8,4,32,16]{2,1,0,3:T(4,128)}) async-done(((f32[240,2048]{0,1:T(8,128)}, f32[8,4,32,16]{2,1,0,3:T(4,128)}), (f32[240,2048]{0,1:T(8,128)}, f32[8,4,32,16]{2,1,0,3:T(4,128)})) %all-reduce.6.cloned.1.call-update) | async-done | bytes 2031632 | tf_op jit(solution)/shard_map/psum | solution.py:262
  599.5 3.4 fusion.227
  612.9 3.0 fusion.82
  620.9 6.2 collective-permute-done.9
  628.6 4.3 collective-permute-done.11
  633.6 2.5 fusion.83
  636.1 4.2 fusion.84
  640.3 3.6 pad_maximum_fusion.1
  646.6 17.5 %collective-permute-done.12 = bf16[128,1024]{1,0:T(8,128)(2,1)S(1)} collective-permute-done((bf16[128,1024]{1,0:T(8,128)(2,1)S(1)}, bf16[128,1024]{1,0:T(8,128)(2,1)S(1)}, u32[]{:S(2)}, u32[]{:S(2)}) %collective-permute-start.12) | collective-permute-done | bytes 262176 | tf_op jit(solution)/shard_map/ppermute | solution.py:33
  667.3 5.3 collective-permute-done.14
  676.3 24.4 %collective-permute-done.20 = bf16[128,1024]{1,0:T(8,128)(2,1)S(1)} collective-permute-done((bf16[128,1024]{1,0:T(8,128)(2,1)S(1)}, bf16[128,1024]{1,0:T(8,128)(2,1)S(1)}, u32[]{:S(2)}, u32[]{:S(2)}) %collective-permute-start.20) | collective-permute-done | bytes 262176 | tf_op jit(solution)/shard_map/ppermute | solution.py:33
  704.9 10.7 %collective-permute-done.22 = bf16[128,4096]{1,0:T(8,128)(2,1)S(1)} collective-permute-done((bf16[128,4096]{1,0:T(8,128)(2,1)S(1)}, bf16[128,4096]{1,0:T(8,128)(2,1)S(1)}, u32[]{:S(2)}, u32[]{:S(2)}) %collective-permute-start.22) | collective-permute-done | bytes 1048608 | tf_op jit(solution)/shard_map/ppermute | solution.py:36
  716.6 3.8 collective-permute-done.17
  721.5 6.7 fusion.85
  728.2 3.5 collective-permute-done.23
  732.7 6.8 fusion.86
  739.5 7.8 pad_maximum_fusion
  754.4 82.6 %reduce-scatter.9.cloned.1.call-done = f32[32,4096]{1,0:T(8,128)} async-done(((f32[256,4096]{1,0:T(8,128)}), f32[32,4096]{1,0:T(8,128)}) %reduce-scatter.9.cloned.1.call-update) | async-done | bytes 524304 | tf_op jit(solution)/shard_map/reduce_scatter | solution.py:308
  840.1 149.2 %reduce-scatter.11.cloned.1.call-done = f32[32,8192]{1,0:T(8,128)} async-done(((f32[256,8192]{1,0:T(8,128)}), f32[32,8192]{1,0:T(8,128)}) %reduce-scatter.11.cloned.1.call-update) | async-done | bytes 1048592 | tf_op jit(solution)/shard_map/reduce_scatter | solution.py:308
  993.3 39.3 %all-reduce.2 = (f32[]{:T(128)}, f32[]{:T(128)}) all-reduce(f32[]{:T(128)} %get-tuple-element.167, f32[]{:T(128)S(6)} %add.424), channel_id=1, replica_groups=mesh['dp'=8,'fsdp'=4] {'dp','fsdp'}, use_global_device_ids=true, to_apply=%region_13.14 | all-reduce | flops 2 | bytes 16 | tf_op jit(solution)/shard_map/psum | solution.py:216
  1038.1 3.8 fusion.211
  (412 shorter events, 140.2 us)
Async XLA Ops:
  7.2 82.3 %all-gather.6.cloned.1.call-start = ((), (), s32[]{:S(2)}) async-start(), calls=%async_computation.5 | async-start | bytes 8110080 | tf_op jit(solution)/shard_map/all_gather | solution.py:153
  10.8 158.2 %all-gather.8.cloned.1.call-start = ((), (), s32[]{:S(2)}) async-start(), calls=%async_computation.6 | async-start | bytes 8650752 | tf_op jit(solution)/shard_map/all_gather | solution.py:154
  13.3 90.0 %copy-start.71 = (pred[240]{0:T(512)(128)(4,1)}, pred[240]{0:T(512)(128)(4,1)S(1)}, u32[]{:S(2)}) copy-start(pred[240]{0:T(512)(128)(4,1)S(1)} %iota_compare_fusion.5) | copy-start | bytes 724
  14.0 89.3 %copy-start.59 = (s32[240]{0:T(256)}, s32[240]{0:T(256)S(1)}, u32[]{:S(2)}) copy-start(s32[240]{0:T(256)S(1)} %get-tuple-element.240) | copy-start | bytes 2884
  14.0 89.3 %copy-start.61 = (s32[240]{0:T(256)}, s32[240]{0:T(256)S(1)}, u32[]{:S(2)}) copy-start(s32[240]{0:T(256)S(1)} %get-tuple-element.241) | copy-start | bytes 2884
  14.8 90.2 %copy-start.14 = (f32[240,128]{1,0:T(8,128)}, f32[240,128]{1,0:T(8,128)S(1)}, u32[]{:S(2)}) copy-start(f32[240,128]{1,0:T(8,128)S(1)} %pad_convert_fusion) | copy-start | bytes 368644
  16.3 84.6 %copy-start.64 = (s32[128]{0:T(128)}, s32[128]{0:T(128)S(1)}, u32[]{:S(2)}) copy-start(s32[128]{0:T(128)S(1)} %add_subtract_fusion) | copy-start | bytes 1540
  178.5 15.9 %all-to-all-start = ((bf16[128,3,4,256]{3,0,1,2:T(8,128)(2,1)}), bf16[128,3,4,256]{3,0,1,2:T(8,128)(2,1)}, u32[]{:S(2)}, u32[]{:S(2)}) async-start(bf16[128,3,4,256]{3,0,1,2:T(8,128)(2,1)} %copy.206), calls=%async_computation | async-start | bytes 1572864 | tf_op jit(solution)/shard_map/all_to_all | solution.py:190
  182.7 40.6 %all-gather.10.cloned.1.call-start = ((), (), s32[]{:S(2)}) async-start(), calls=%async_computation.7 | async-start | bytes 1310720 | tf_op jit(solution)/shard_map/all_gather | solution.py:204
  207.8 19.1 %copy-start.58 = (f32[1,1024]{1,0:T(1,128)S(1)}, f32[1,1024]{1,0:T(1,128)}, u32[]{:S(2)}) copy-start(f32[1,1024]{1,0:T(1,128)} %get-tuple-element.217) | copy-start | bytes 12292
  207.9 133.6 %all-gather.12.cloned.1.call-start = ((), (), s32[]{:S(2)}) async-start(), calls=%async_computation.8 | async-start | bytes 17301504 | tf_op jit(solution)/shard_map/all_gather | solution.py:155
  210.0 302.3 %all-gather.14.cloned.1.call-start = ((), (), s32[]{:S(2)}) async-start(), calls=%async_computation.9 | async-start | bytes 3932160 | tf_op jit(solution)/shard_map/all_gather | solution.py:241
  344.0 15.9 %slice-start = ((s8[7864320]{0:T(1024)(128)(4,1)}), s8[4194304]{0:T(1024)(128)(4,1)S(1)}, s32[]{:S(2)}) async-start(s8[7864320]{0:T(1024)(128)(4,1)} %bitcast.187), calls=%async_computation.15 | async-start | bytes 8388608
  429.2 6.3 collective-permute-start
  429.2 10.9 %collective-permute-start.1 = (bf16[128,1024]{1,0:T(8,128)(2,1)}, bf16[128,1024]{1,0:T(8,128)(2,1)}, u32[]{:S(2)}, u32[]{:S(2)}) collective-permute-start(bf16[128,1024]{1,0:T(8,128)(2,1)} %get-tuple-element.210), channel_id=1, source_target_pairs={{0,3},{1,0},{2,1},{3,2},{4,7},{5,4},{6,5},{7,6},{8,11},{9,8},{10,9... | collective-permute-start | bytes 786440 | tf_op jit(solution)/shard_map/ppermute | solution.py:36
  435.5 6.1 collective-permute-start.2
  469.2 130.3 %all-reduce.6.cloned.1.call-start = ((), (), s32[]{:S(2)}) async-start(), calls=%async_computation.14 | async-start | bytes 4718592 | tf_op jit(solution)/shard_map/psum | solution.py:262
  470.0 4.0 collective-permute-start.30
  472.3 5.8 collective-permute-start.31
  474.0 5.6 collective-permute-start.32
  482.0 30.3 %copy-start.67 = (f32[128]{0:T(128)S(1)}, f32[128]{0:T(128)}, u32[]{:S(2)}) copy-start(f32[128]{0:T(128)} %copy-done.66) | copy-start | bytes 1540
  482.0 124.0 %collective-permute-start.3 = (bf16[128,1024]{0,1:T(8,128)(2,1)}, bf16[128,1024]{0,1:T(8,128)(2,1)}, u32[]{:S(2)}, u32[]{:S(2)}) collective-permute-start(bf16[128,1024]{0,1:T(8,128)(2,1)} %bitcast.197), channel_id=1, source_target_pairs={{0,1},{1,2},{2,3},{3,0},{4,5},{5,6},{6,7},{7,4},{8,9},{9,10},{10,1... | collective-permute-start | bytes 786440 | tf_op jit(solution)/shard_map/ppermute | solution.py:33
  484.4 124.6 %collective-permute-start.4 = (bf16[128,1024]{0,1:T(8,128)(2,1)}, bf16[128,1024]{0,1:T(8,128)(2,1)}, u32[]{:S(2)}, u32[]{:S(2)}) collective-permute-start(bf16[128,1024]{0,1:T(8,128)(2,1)} %bitcast.198), channel_id=1, source_target_pairs={{0,3},{1,0},{2,1},{3,2},{4,7},{5,4},{6,5},{7,6},{8,11},{9,8},{10,9... | collective-permute-start | bytes 786440 | tf_op jit(solution)/shard_map/ppermute | solution.py:36
  484.4 12.7 %collective-permute-start.27 = (bf16[128,192]{0,1:T(8,128)(2,1)S(1)}, bf16[128,192]{0,1:T(8,128)(2,1)S(1)}, u32[]{:S(2)}, u32[]{:S(2)}) collective-permute-start(bf16[128,192]{0,1:T(8,128)(2,1)S(1)} %copy-done.50), channel_id=1, source_target_pairs={{0,1},{1,2},{2,3},{3,0},{4,5},{5,6},{6,7},{7,4},{8,9},{9,10},{10,1... | collective-permute-start | bytes 147464 | tf_op jit(solution)/shard_map/ppermute | solution.py:33
  487.1 11.5 %collective-permute-start.28 = (bf16[128,192]{0,1:T(8,128)(2,1)S(1)}, bf16[128,192]{0,1:T(8,128)(2,1)S(1)}, u32[]{:S(2)}, u32[]{:S(2)}) collective-permute-start(bf16[128,192]{0,1:T(8,128)(2,1)S(1)} %copy-done.50), channel_id=1, source_target_pairs={{0,3},{1,0},{2,1},{3,2},{4,7},{5,4},{6,5},{7,6},{8,11},{9,8},{10,9... | collective-permute-start | bytes 147464 | tf_op jit(solution)/shard_map/ppermute | solution.py:36
  487.2 23.4 %collective-permute-start.24 = (bf16[128,1024]{1,0:T(8,128)(2,1)}, bf16[128,1024]{1,0:T(8,128)(2,1)}, u32[]{:S(2)}, u32[]{:S(2)}) collective-permute-start(bf16[128,1024]{1,0:T(8,128)(2,1)} %get-tuple-element.193), channel_id=1, source_target_pairs={{0,1},{1,2},{2,3},{3,0},{4,5},{5,6},{6,7},{7,4},{8,9},{9,10},{10,1... | collective-permute-start | bytes 786440 | tf_op jit(solution)/shard_map/ppermute | solution.py:33
  497.1 41.7 %collective-permute-start.25 = (bf16[128,1024]{1,0:T(8,128)(2,1)}, bf16[128,1024]{1,0:T(8,128)(2,1)}, u32[]{:S(2)}, u32[]{:S(2)}) collective-permute-start(bf16[128,1024]{1,0:T(8,128)(2,1)} %get-tuple-element.193), channel_id=1, source_target_pairs={{0,3},{1,0},{2,1},{3,2},{4,7},{5,4},{6,5},{7,6},{8,11},{9,8},{10,9... | collective-permute-start | bytes 786440 | tf_op jit(solution)/shard_map/ppermute | solution.py:36
  498.7 11.3 %collective-permute-start.29 = (bf16[128,192]{0,1:T(8,128)(2,1)S(1)}, bf16[128,192]{0,1:T(8,128)(2,1)S(1)}, u32[]{:S(2)}, u32[]{:S(2)}) collective-permute-start(bf16[128,192]{0,1:T(8,128)(2,1)S(1)} %collective-permute-done.27), channel_id=1, source_target_pairs={{0,1},{1,2},{2,3},{3,0},{4,5},{5,6},{6,7},{7,4},{8,9},{9,10},{10,1... | collective-permute-start | bytes 147464 | tf_op jit(solution)/shard_map/ppermute | solution.py:33
  510.6 29.9 %collective-permute-start.26 = (bf16[128,1024]{1,0:T(8,128)(2,1)}, bf16[128,1024]{1,0:T(8,128)(2,1)}, u32[]{:S(2)}, u32[]{:S(2)}) collective-permute-start(bf16[128,1024]{1,0:T(8,128)(2,1)} %collective-permute-done.24), channel_id=1, source_target_pairs={{0,1},{1,2},{2,3},{3,0},{4,5},{5,6},{6,7},{7,4},{8,9},{9,10},{10,1... | collective-permute-start | bytes 786440 | tf_op jit(solution)/shard_map/ppermute | solution.py:33
  527.6 14.6 %collective-permute-start.6 = (bf16[128,1024]{1,0:T(8,128)(2,1)}, bf16[128,1024]{1,0:T(8,128)(2,1)S(1)}, u32[]{:S(2)}, u32[]{:S(2)}) collective-permute-start(bf16[128,1024]{1,0:T(8,128)(2,1)} %get-tuple-element.208), channel_id=1, source_target_pairs={{0,1},{1,2},{2,3},{3,0},{4,5},{5,6},{6,7},{7,4},{8,9},{9,10},{10,1... | collective-permute-start | bytes 786440 | tf_op jit(solution)/shard_map/ppermute | solution.py:33
  538.7 60.8 %copy-start.7 = (bf16[8,1,32,2048]{3,2,1,0:T(8,128)(2,1)S(1)}, bf16[8,1,32,2048]{3,2,1,0:T(8,128)(2,1)}, u32[]{:S(2)}) copy-start(bf16[8,1,32,2048]{3,2,1,0:T(8,128)(2,1)} %constant_dynamic-slice_fusion) | copy-start | bytes 3145732
  538.7 209.4 %reduce-scatter.13.cloned.1.call-start = ((), (), s32[]{:S(2)}) async-start(), calls=%async_computation.13 | async-start | bytes 884736 | tf_op jit(solution)/shard_map/reduce_scatter | solution.py:308
  542.2 11.2 %collective-permute-start.7 = (bf16[128,1024]{1,0:T(8,128)(2,1)}, bf16[128,1024]{1,0:T(8,128)(2,1)S(1)}, u32[]{:S(2)}, u32[]{:S(2)}) collective-permute-start(bf16[128,1024]{1,0:T(8,128)(2,1)} %get-tuple-element.208), channel_id=1, source_target_pairs={{0,3},{1,0},{2,1},{3,2},{4,7},{5,4},{6,5},{7,6},{8,11},{9,8},{10,9... | collective-permute-start | bytes 786440 | tf_op jit(solution)/shard_map/ppermute | solution.py:36
  542.2 13.2 %collective-permute-start.8 = (bf16[128,1024]{1,0:T(8,128)(2,1)S(1)}, bf16[128,1024]{1,0:T(8,128)(2,1)S(1)}, u32[]{:S(2)}, u32[]{:S(2)}) collective-permute-start(bf16[128,1024]{1,0:T(8,128)(2,1)S(1)} %collective-permute-done.6), channel_id=1, source_target_pairs={{0,1},{1,2},{2,3},{3,0},{4,5},{5,6},{6,7},{7,4},{8,9},{9,10},{10,1... | collective-permute-start | bytes 786440 | tf_op jit(solution)/shard_map/ppermute | solution.py:33
  555.5 44.0 %copy-start.27 = (bf16[512,1024]{1,0:T(8,128)(2,1)}, bf16[512,1024]{1,0:T(8,128)(2,1)S(1)}, u32[]{:S(2)}) copy-start(bf16[512,1024]{1,0:T(8,128)(2,1)S(1)} %constant_dynamic-update-slice_fusion.31) | copy-start | bytes 3145732
  605.7 147.0 %reduce-scatter.7.cloned.1.call-start = ((), (), s32[]{:S(2)}) async-start(), calls=%async_computation.10 | async-start | bytes 3538944 | tf_op jit(solution)/shard_map/reduce_scatter | solution.py:308
  606.0 6.1 collective-permute-start.5
  617.2 16.5 %copy-start.24 = (bf16[512,1024]{1,0:T(8,128)(2,1)S(1)}, bf16[512,1024]{1,0:T(8,128)(2,1)}, u32[]{:S(2)}) copy-start(bf16[512,1024]{1,0:T(8,128)(2,1)} %copy-done.23) | copy-start | bytes 3145732
  619.0 14.6 %copy-start.47 = (bf16[512,1024]{0,1:T(8,128)(2,1)S(1)}, bf16[512,1024]{0,1:T(8,128)(2,1)}, u32[]{:S(2)}) copy-start(bf16[512,1024]{0,1:T(8,128)(2,1)} %all-gather.10.cloned.1.call-done) | copy-start | bytes 3145732
  619.0 218.0 %reduce-scatter.9.cloned.1.call-start = ((), (), s32[]{:S(2)}) async-start(), calls=%async_computation.11 | async-start | bytes 4718592 | tf_op jit(solution)/shard_map/reduce_scatter | solution.py:308
  619.1 8.0 collective-permute-start.9
  619.2 8.7 collective-permute-start.10
  627.1 5.8 collective-permute-start.11
  643.9 22.7 %copy-start.87 = (bf16[128,4096]{1,0:T(8,128)(2,1)S(1)}, bf16[128,4096]{1,0:T(8,128)(2,1)}, u32[]{:S(2)}) copy-start(bf16[128,4096]{1,0:T(8,128)(2,1)} %copy-done.86) | copy-start | bytes 3145732
  643.9 345.4 %reduce-scatter.11.cloned.1.call-start = ((), (), s32[]{:S(2)}) async-start(), calls=%async_computation.12 | async-start | bytes 9437184 | tf_op jit(solution)/shard_map/reduce_scatter | solution.py:308
  644.0 57.4 %collective-permute-start.15 = (bf16[128,4096]{1,0:T(8,128)(2,1)}, bf16[128,4096]{1,0:T(8,128)(2,1)S(1)}, u32[]{:S(2)}, u32[]{:S(2)}) collective-permute-start(bf16[128,4096]{1,0:T(8,128)(2,1)} %copy-done.88), channel_id=1, source_target_pairs={{0,1},{1,2},{2,3},{3,0},{4,5},{5,6},{6,7},{7,4},{8,9},{9,10},{10,1... | collective-permute-start | bytes 3145736 | tf_op jit(solution)/shard_map/ppermute | solution.py:33
  644.8 19.2 %collective-permute-start.12 = (bf16[128,1024]{1,0:T(8,128)(2,1)S(1)}, bf16[128,1024]{1,0:T(8,128)(2,1)S(1)}, u32[]{:S(2)}, u32[]{:S(2)}) collective-permute-start(bf16[128,1024]{1,0:T(8,128)(2,1)S(1)} %copy-done.38), channel_id=1, source_target_pairs={{0,1},{1,2},{2,3},{3,0},{4,5},{5,6},{6,7},{7,4},{8,9},{9,10},{10,1... | collective-permute-start | bytes 786440 | tf_op jit(solution)/shard_map/ppermute | solution.py:33
  644.9 21.7 %collective-permute-start.13 = (bf16[128,1024]{1,0:T(8,128)(2,1)S(1)}, bf16[128,1024]{1,0:T(8,128)(2,1)S(1)}, u32[]{:S(2)}, u32[]{:S(2)}) collective-permute-start(bf16[128,1024]{1,0:T(8,128)(2,1)S(1)} %copy-done.38), channel_id=1, source_target_pairs={{0,3},{1,0},{2,1},{3,2},{4,7},{5,4},{6,5},{7,6},{8,11},{9,8},{10,9... | collective-permute-start | bytes 786440 | tf_op jit(solution)/shard_map/ppermute | solution.py:36
  646.6 20.7 %collective-permute-start.18 = (bf16[128,1024]{1,0:T(8,128)(2,1)S(1)}, bf16[128,1024]{1,0:T(8,128)(2,1)S(1)}, u32[]{:S(2)}, u32[]{:S(2)}) collective-permute-start(bf16[128,1024]{1,0:T(8,128)(2,1)S(1)} %copy-done.43), channel_id=1, source_target_pairs={{0,1},{1,2},{2,3},{3,0},{4,5},{5,6},{6,7},{7,4},{8,9},{9,10},{10,1... | collective-permute-start | bytes 786440 | tf_op jit(solution)/shard_map/ppermute | solution.py:33
  664.1 8.5 collective-permute-start.14
  664.8 9.2 collective-permute-start.19
  666.6 36.2 %collective-permute-start.21 = (bf16[128,4096]{1,0:T(8,128)(2,1)S(1)}, bf16[128,4096]{1,0:T(8,128)(2,1)S(1)}, u32[]{:S(2)}, u32[]{:S(2)}) collective-permute-start(bf16[128,4096]{1,0:T(8,128)(2,1)S(1)} %copy-done.87), channel_id=1, source_target_pairs={{0,1},{1,2},{2,3},{3,0},{4,5},{5,6},{6,7},{7,4},{8,9},{9,10},{10,1... | collective-permute-start | bytes 3145736 | tf_op jit(solution)/shard_map/ppermute | solution.py:33
  667.3 33.4 %collective-permute-start.20 = (bf16[128,1024]{1,0:T(8,128)(2,1)S(1)}, bf16[128,1024]{1,0:T(8,128)(2,1)S(1)}, u32[]{:S(2)}, u32[]{:S(2)}) collective-permute-start(bf16[128,1024]{1,0:T(8,128)(2,1)S(1)} %collective-permute-done.18), channel_id=1, source_target_pairs={{0,1},{1,2},{2,3},{3,0},{4,5},{5,6},{6,7},{7,4},{8,9},{9,10},{10,1... | collective-permute-start | bytes 786440 | tf_op jit(solution)/shard_map/ppermute | solution.py:33
  673.3 30.5 %collective-permute-start.16 = (bf16[128,4096]{1,0:T(8,128)(2,1)}, bf16[128,4096]{1,0:T(8,128)(2,1)S(1)}, u32[]{:S(2)}, u32[]{:S(2)}) collective-permute-start(bf16[128,4096]{1,0:T(8,128)(2,1)} %copy-done.88), channel_id=1, source_target_pairs={{0,3},{1,0},{2,1},{3,2},{4,7},{5,4},{6,5},{7,6},{8,11},{9,8},{10,9... | collective-permute-start | bytes 3145736 | tf_op jit(solution)/shard_map/ppermute | solution.py:36
  674.0 41.6 %collective-permute-start.22 = (bf16[128,4096]{1,0:T(8,128)(2,1)S(1)}, bf16[128,4096]{1,0:T(8,128)(2,1)S(1)}, u32[]{:S(2)}, u32[]{:S(2)}) collective-permute-start(bf16[128,4096]{1,0:T(8,128)(2,1)S(1)} %copy-done.87), channel_id=1, source_target_pairs={{0,3},{1,0},{2,1},{3,2},{4,7},{5,4},{6,5},{7,6},{8,11},{9,8},{10,9... | collective-permute-start | bytes 3145736 | tf_op jit(solution)/shard_map/ppermute | solution.py:36
  701.4 19.0 %collective-permute-start.17 = (bf16[128,4096]{1,0:T(8,128)(2,1)S(1)}, bf16[128,4096]{1,0:T(8,128)(2,1)S(1)}, u32[]{:S(2)}, u32[]{:S(2)}) collective-permute-start(bf16[128,4096]{1,0:T(8,128)(2,1)S(1)} %collective-permute-done.15), channel_id=1, source_target_pairs={{0,1},{1,2},{2,3},{3,0},{4,5},{5,6},{6,7},{7,4},{8,9},{9,10},{10,1... | collective-permute-start | bytes 3145736 | tf_op jit(solution)/shard_map/ppermute | solution.py:33
  702.7 29.0 %collective-permute-start.23 = (bf16[128,4096]{1,0:T(8,128)(2,1)S(1)}, bf16[128,4096]{1,0:T(8,128)(2,1)S(1)}, u32[]{:S(2)}, u32[]{:S(2)}) collective-permute-start(bf16[128,4096]{1,0:T(8,128)(2,1)S(1)} %collective-permute-done.21), channel_id=1, source_target_pairs={{0,1},{1,2},{2,3},{3,0},{4,5},{5,6},{6,7},{7,4},{8,9},{9,10},{10,1... | collective-permute-start | bytes 3145736 | tf_op jit(solution)/shard_map/ppermute | solution.py:33
  747.2 287.5 %copy-start.54 = (f32[32,9]{0,1:T(8,128)S(1)}, f32[32,9]{0,1:T(8,128)}, u32[]{:S(2)}) copy-start(f32[32,9]{0,1:T(8,128)} %param.35) | copy-start | bytes 3460
  747.3 288.9 %copy-start.44 = (f32[32,944]{1,0:T(8,128)S(1)}, f32[32,944]{1,0:T(8,128)}, u32[]{:S(2)}) copy-start(f32[32,944]{1,0:T(8,128)} %param.34) | copy-start | bytes 362500
  747.3 288.9 %copy-start.45 = (f32[32,944]{1,0:T(8,128)S(1)}, f32[32,944]{1,0:T(8,128)}, u32[]{:S(2)}) copy-start(f32[32,944]{1,0:T(8,128)} %param.44) | copy-start | bytes 362500
  747.3 288.9 %copy-start.46 = (f32[32,944]{1,0:T(8,128)S(1)}, f32[32,944]{1,0:T(8,128)}, u32[]{:S(2)}) copy-start(f32[32,944]{1,0:T(8,128)} %param.39) | copy-start | bytes 362500
  747.3 290.8 %copy-start.8 = (f32[32,8192]{1,0:T(8,128)S(1)}, f32[32,8192]{1,0:T(8,128)}, u32[]{:S(2)}) copy-start(f32[32,8192]{1,0:T(8,128)} %param.33) | copy-start | bytes 3145732
  747.3 290.7 %copy-start.18 = (f32[32,8192]{1,0:T(8,128)S(1)}, f32[32,8192]{1,0:T(8,128)}, u32[]{:S(2)}) copy-start(f32[32,8192]{1,0:T(8,128)} %param.43) | copy-start | bytes 3145732
  747.3 290.7 %copy-start.19 = (f32[32,8192]{1,0:T(8,128)S(1)}, f32[32,8192]{1,0:T(8,128)}, u32[]{:S(2)}) copy-start(f32[32,8192]{1,0:T(8,128)} %param.38) | copy-start | bytes 3145732
  (75 other events, 380.3 us)
Sparse Core Ops, SparseCore 0:
  11.5 77.9 all-gather.5
  92.9 76.0 all-gather.7
  208.0 15.2 all-gather.9
  226.6 114.8 all-gather.11
  469.3 42.9 all-gather.13
  538.9 60.5 all-reduce.5
  605.8 62.5 reduce-scatter.12
  672.5 73.3 reduce-scatter.6
  750.0 87.0 reduce-scatter.8
  840.5 148.7 reduce-scatter.10
